TPU v7x, 32 devices: a whole 2x2x4 slice. The times are simulated.
32 devices in a mesh: dp: 8 (over z, y), tensor: 4 (over x, core).
Axes of the slice: x: 2, y: 2, z: 4, core: 2. Of those that a mesh axis runs over, the one named last changes fastest.
Arguments:
- tokens: bfloat16 [16384, 768], P(('dp', 'tensor')), may hold values from -6 to 6
- segments: int32 [8, 2048], P('dp', 'tensor'), may hold values from 0 to 3, never falling along the last dimension, each value on 1 to 1024 neighbouring positions
- query_proj: bfloat16 [768, 768], P('dp', 'tensor'), may hold values from -0.3125 to 0.3125
- query_bias: float32 [768], P(('dp', 'tensor')), may hold values from -3 to 3
- key_proj: bfloat16 [768, 768], P('dp', 'tensor'), may hold values from -0.21875 to 0.21875
- value_proj: bfloat16 [768, 768], P('dp', 'tensor'), may hold values from -0.21875 to 0.21875
- value_bias: float32 [768], P(('dp', 'tensor')), may hold values from -3 to 3
- merge_proj: bfloat16 [768, 768], P('tensor', 'dp'), may hold values from -1.75 to 1.75
- merge_bias: float32 [768], P(('dp', 'tensor')), may hold values from -3 to 3
- first_gain: float32 [768], P(('dp', 'tensor')), may hold values from 0.5 to 1.5
- first_shift: float32 [768], P(('dp', 'tensor')), may hold values from -3 to 3
- expand_proj: bfloat16 [768, 3072], P('dp', 'tensor'), may hold values from -0.21875 to 0.21875
- expand_bias: float32 [3072], P(('dp', 'tensor')), may hold values from -3 to 3
- shrink_proj: bfloat16 [3072, 768], P('tensor', 'dp'), may hold values from -0.15625 to 0.15625
- shrink_bias: float32 [768], P(('dp', 'tensor')), may hold values from -3 to 3
- second_gain: float32 [768], P(('dp', 'tensor')), may hold values from 0.5 to 1.5
- second_shift: float32 [768], P(('dp', 'tensor')), may hold values from -3 to 3
- cotangent: bfloat16 [16384, 768], P(('dp', 'tensor')), may hold values from -6 to 6
Outputs:
- output: bfloat16 [16384, 768], P(('dp', 'tensor'))
- tokens_grad: bfloat16 [16384, 768], P(('dp', 'tensor'))
- querygrad: float32 [768, 768], P('dp', 'tensor')
- qbiasgrad: float32 [768], P(('dp', 'tensor'))
- keygrad: float32 [768, 768], P('dp', 'tensor')
- valuegrad: float32 [768, 768], P('dp', 'tensor')
- vbiasgrad: float32 [768], P(('dp', 'tensor'))
- mergegrad: float32 [768, 768], P('tensor', 'dp')
- mbiasgrad: float32 [768], P(('dp', 'tensor'))
- fgaingrad: float32 [768], P(('dp', 'tensor'))
- fshiftgrad: float32 [768], P(('dp', 'tensor'))
- expandgrad: float32 [768, 3072], P('dp', 'tensor')
- ebiasgrad: float32 [3072], P(('dp', 'tensor'))
- shrinkgrad: float32 [3072, 768], P('tensor', 'dp')
- sbiasgrad: float32 [768], P(('dp', 'tensor'))
- sgaingrad: float32 [768], P(('dp', 'tensor'))
- sshiftgrad: float32 [768], P(('dp', 'tensor'))
Inputs may be any that keep to these rules, and one draw needn't show every extreme that they name: `segments`: along each sequence the segment numbers never fall; each of the 4 numbers marks 1 to 1024 positions of every sequence.
All inputs are finite; a program needn't handle non-finite values.
Results may differ from a plain program's by a relative error of at most 0.023.
Values may be sent and summed in bfloat16 or wider, within the bound.
No kernel may reach another device: no remote copies, remote signals or barrier semaphores. Data moves between devices by JAX's collectives and lax.ppermute only.
A program may use at most 128 MiB of HBM per device.

v0:
```python
import jax
import jax.numpy as jnp
from jax import lax
from jax.sharding import PartitionSpec as P

HD = 64
EPSILON = 1e-12
CONTRACT_ROWS = (((0,), (0,)), ((), ()))
CONTRACT_COLUMNS = (((1,), (1,)), ((), ()))


def normalize(values, gain, shift):
    centre = jnp.mean(values, axis=-1, keepdims=True)
    centred = values - centre
    spread = jnp.mean(centred * centred, axis=-1, keepdims=True)
    return centred * lax.rsqrt(spread + EPSILON) * gain + shift


def gelu_exact(values):
    return jax.nn.gelu(values, approximate=False)


def assemble(pieces, count, heads):
    block = pieces.shape[1]
    depth = pieces.shape[2]
    return (
        pieces.reshape(count, heads, block, depth)
        .transpose(0, 2, 1, 3)
        .reshape(count * block, heads * depth)
    )


def attend(query, keys, values, seg_row, depth):
    length, width = query.shape
    heads = width // depth
    block = min(512, length)
    count = length // block
    scale = depth ** (-0.5)

    def one(index):
        start = index // heads * block
        column = index % heads * depth
        query_rows = lax.dynamic_slice(query, (start, column), (block, depth))
        key_head = lax.dynamic_slice(keys, (0, column), (length, depth))
        value_head = lax.dynamic_slice(values, (0, column), (length, depth))
        seg_rows = lax.dynamic_slice_in_dim(seg_row, start, block)
        scores = (
            lax.dot_general(
                query_rows, key_head, CONTRACT_COLUMNS, preferred_element_type=jnp.float32
            )
            * scale
        )
        scores = jnp.where(seg_rows[:, None] == seg_row[None, :], scores, -1e30)
        peak = jnp.max(scores, axis=1, keepdims=True)
        raised = jnp.exp(scores - peak)
        total = jnp.sum(raised, axis=1, keepdims=True)
        chance = (raised / total).astype(jnp.bfloat16)
        context = jnp.dot(chance, value_head, preferred_element_type=jnp.float32)
        return (context, (peak + jnp.log(total))[:, 0])

    contexts, logsum = lax.map(one, jnp.arange(count * heads))
    return (assemble(contexts, count, heads), logsum)


def attend_back(query, keys, values, grad_context, logsum, seg_row, depth):
    length, width = query.shape
    heads = width // depth
    block = min(512, length)
    count = length // block
    scale = depth ** (-0.5)

    def one(carry, index):
        grad_keys, grad_values = carry
        start = index // heads * block
        column = index % heads * depth
        query_rows = lax.dynamic_slice(query, (start, column), (block, depth))
        grad_rows = lax.dynamic_slice(grad_context, (start, column), (block, depth))
        key_head = lax.dynamic_slice(keys, (0, column), (length, depth))
        value_head = lax.dynamic_slice(values, (0, column), (length, depth))
        seg_rows = lax.dynamic_slice_in_dim(seg_row, start, block)
        scores = (
            lax.dot_general(
                query_rows, key_head, CONTRACT_COLUMNS, preferred_element_type=jnp.float32
            )
            * scale
        )
        scores = jnp.where(seg_rows[:, None] == seg_row[None, :], scores, -1e30)
        chance = jnp.exp(scores - logsum[index][:, None])
        grad_chance = lax.dot_general(
            grad_rows, value_head, CONTRACT_COLUMNS, preferred_element_type=jnp.float32
        )
        inner = jnp.sum(chance * grad_chance, axis=1, keepdims=True)
        grad_scores = (chance * (grad_chance - inner) * scale).astype(jnp.bfloat16)
        grad_query = jnp.dot(grad_scores, key_head, preferred_element_type=jnp.float32)
        key_part = lax.dot_general(
            grad_scores, query_rows, CONTRACT_ROWS, preferred_element_type=jnp.float32
        )
        value_part = lax.dot_general(
            chance.astype(jnp.bfloat16),
            grad_rows,
            CONTRACT_ROWS,
            preferred_element_type=jnp.float32,
        )
        old_keys = lax.dynamic_slice(grad_keys, (0, column), (length, depth))
        old_values = lax.dynamic_slice(grad_values, (0, column), (length, depth))
        grad_keys = lax.dynamic_update_slice(grad_keys, old_keys + key_part, (0, column))
        grad_values = lax.dynamic_update_slice(grad_values, old_values + value_part, (0, column))
        return ((grad_keys, grad_values), grad_query)

    empty = jnp.zeros((length, width), jnp.float32)
    (grad_keys, grad_values), grad_queries = lax.scan(
        one, (empty, empty), jnp.arange(count * heads)
    )
    return (assemble(grad_queries, count, heads), grad_keys, grad_values)


def widen(local, full_size, offset):
    return lax.dynamic_update_slice_in_dim(jnp.zeros((full_size,), jnp.float32), local, offset, 0)


def on_device(
    tokens,
    segments,
    query_proj,
    query_bias,
    key_proj,
    value_proj,
    value_bias,
    merge_proj,
    merge_bias,
    first_gain,
    first_shift,
    expand_proj,
    expand_bias,
    shrink_proj,
    shrink_bias,
    second_gain,
    second_shift,
    cotangent,
):
    part = lax.axis_index("tensor")
    query_full, key_full, value_full, merge_full, expand_full, shrink_full = (
        lax.all_gather(query_proj, "dp", axis=0, tiled=True),
        lax.all_gather(key_proj, "dp", axis=0, tiled=True),
        lax.all_gather(value_proj, "dp", axis=0, tiled=True),
        lax.all_gather(merge_proj, "dp", axis=1, tiled=True),
        lax.all_gather(expand_proj, "dp", axis=0, tiled=True),
        lax.all_gather(shrink_proj, "dp", axis=1, tiled=True),
    )
    (
        bias_query,
        bias_value,
        bias_merge,
        gain_first,
        shift_first,
        bias_expand,
        bias_shrink,
        gain_second,
        shift_second,
    ) = (
        lax.all_gather(query_bias, ("dp", "tensor"), axis=0, tiled=True),
        lax.all_gather(value_bias, ("dp", "tensor"), axis=0, tiled=True),
        lax.all_gather(merge_bias, ("dp", "tensor"), axis=0, tiled=True),
        lax.all_gather(first_gain, ("dp", "tensor"), axis=0, tiled=True),
        lax.all_gather(first_shift, ("dp", "tensor"), axis=0, tiled=True),
        lax.all_gather(expand_bias, ("dp", "tensor"), axis=0, tiled=True),
        lax.all_gather(shrink_bias, ("dp", "tensor"), axis=0, tiled=True),
        lax.all_gather(second_gain, ("dp", "tensor"), axis=0, tiled=True),
        lax.all_gather(second_shift, ("dp", "tensor"), axis=0, tiled=True),
    )
    width = query_full.shape[1]
    units = expand_full.shape[1]
    model_width = bias_query.shape[0]
    unit_count = bias_expand.shape[0]
    local_query_bias = lax.dynamic_slice_in_dim(bias_query, part * width, width)
    local_value_bias = lax.dynamic_slice_in_dim(bias_value, part * width, width)
    local_expand_bias = lax.dynamic_slice_in_dim(bias_expand, part * units, units)
    full_tokens, full_segments = (
        lax.all_gather(tokens, "tensor", axis=0, tiled=True),
        lax.all_gather(segments, "tensor", axis=1, tiled=True),
    )
    seg_row = full_segments[0]
    query = (
        jnp.dot(full_tokens, query_full, preferred_element_type=jnp.float32) + local_query_bias
    ).astype(jnp.bfloat16)
    keys = jnp.dot(full_tokens, key_full, preferred_element_type=jnp.float32).astype(jnp.bfloat16)
    values = (
        jnp.dot(full_tokens, value_full, preferred_element_type=jnp.float32) + local_value_bias
    ).astype(jnp.bfloat16)
    context, logsum = attend(query, keys, values, seg_row, HD)
    context_low = context.astype(jnp.bfloat16)
    attended = lax.psum_scatter(
        jnp.dot(context_low, merge_full, preferred_element_type=jnp.float32).astype(jnp.bfloat16),
        "tensor",
        scatter_dimension=0,
        tiled=True,
    ).astype(jnp.float32)
    mixed = tokens.astype(jnp.float32) + attended + bias_merge
    hidden = normalize(mixed, gain_first, shift_first)
    full_hidden = lax.all_gather(hidden.astype(jnp.bfloat16), "tensor", axis=0, tiled=True)
    inner = (
        jnp.dot(full_hidden, expand_full, preferred_element_type=jnp.float32) + local_expand_bias
    )
    active = gelu_exact(inner).astype(jnp.bfloat16)
    summed = (
        hidden
        + lax.psum_scatter(
            jnp.dot(active, shrink_full, preferred_element_type=jnp.float32).astype(jnp.bfloat16),
            "tensor",
            scatter_dimension=0,
            tiled=True,
        ).astype(jnp.float32)
        + bias_shrink
    )
    result, pull_second = jax.vjp(normalize, summed, gain_second, shift_second)
    output = result.astype(jnp.bfloat16)
    grad_summed, grad_gain_second, grad_shift_second = pull_second(cotangent.astype(jnp.float32))
    grad_bias_shrink = jnp.sum(grad_summed, axis=0)
    full_grad_summed = lax.all_gather(
        grad_summed.astype(jnp.bfloat16), "tensor", axis=0, tiled=True
    )
    shrink_local = lax.dot_general(
        active, full_grad_summed, CONTRACT_ROWS, preferred_element_type=jnp.float32
    )
    grad_active = lax.dot_general(
        full_grad_summed, shrink_full, CONTRACT_COLUMNS, preferred_element_type=jnp.float32
    )
    grad_inner = jax.vjp(gelu_exact, inner)[1](grad_active)[0]
    expand_bias_term = widen(jnp.sum(grad_inner, axis=0), unit_count, part * units)
    inner_low = grad_inner.astype(jnp.bfloat16)
    expand_local = lax.dot_general(
        full_hidden, inner_low, CONTRACT_ROWS, preferred_element_type=jnp.float32
    )
    grad_hidden = grad_summed + lax.psum_scatter(
        lax.dot_general(
            inner_low, expand_full, CONTRACT_COLUMNS, preferred_element_type=jnp.float32
        ).astype(jnp.bfloat16),
        "tensor",
        scatter_dimension=0,
        tiled=True,
    ).astype(jnp.float32)
    grad_mixed, grad_gain_first, grad_shift_first = jax.vjp(
        normalize, mixed, gain_first, shift_first
    )[1](grad_hidden)
    grad_bias_merge = jnp.sum(grad_mixed, axis=0)
    full_grad_mixed = lax.all_gather(grad_mixed.astype(jnp.bfloat16), "tensor", axis=0, tiled=True)
    merge_local = lax.dot_general(
        context_low, full_grad_mixed, CONTRACT_ROWS, preferred_element_type=jnp.float32
    )
    grad_context = lax.dot_general(
        full_grad_mixed, merge_full, CONTRACT_COLUMNS, preferred_element_type=jnp.float32
    ).astype(jnp.bfloat16)
    grad_query, grad_keys, grad_values = attend_back(
        query, keys, values, grad_context, logsum, seg_row, HD
    )
    grad_bias_query = jnp.sum(grad_query, axis=0)
    grad_bias_value = jnp.sum(grad_values, axis=0)
    query_low = grad_query.astype(jnp.bfloat16)
    key_low = grad_keys.astype(jnp.bfloat16)
    value_low = grad_values.astype(jnp.bfloat16)
    query_local = lax.dot_general(
        full_tokens, query_low, CONTRACT_ROWS, preferred_element_type=jnp.float32
    )
    key_local = lax.dot_general(
        full_tokens, key_low, CONTRACT_ROWS, preferred_element_type=jnp.float32
    )
    value_local = lax.dot_general(
        full_tokens, value_low, CONTRACT_ROWS, preferred_element_type=jnp.float32
    )
    total = lax.dot_general(
        query_low, query_full, CONTRACT_COLUMNS, preferred_element_type=jnp.float32
    )
    total = total + lax.dot_general(
        key_low, key_full, CONTRACT_COLUMNS, preferred_element_type=jnp.float32
    )
    tokens_grad = (
        grad_mixed
        + lax.psum_scatter(
            (
                total
                + lax.dot_general(
                    value_low, value_full, CONTRACT_COLUMNS, preferred_element_type=jnp.float32
                )
            ).astype(jnp.bfloat16),
            "tensor",
            scatter_dimension=0,
            tiled=True,
        ).astype(jnp.float32)
    ).astype(jnp.bfloat16)
    (
        qbiasgrad,
        vbiasgrad,
        mbiasgrad,
        fgaingrad,
        fshiftgrad,
        ebiasgrad,
        sbiasgrad,
        sgaingrad,
        sshiftgrad,
    ) = (
        lax.psum_scatter(
            widen(grad_bias_query, model_width, part * width),
            ("dp", "tensor"),
            scatter_dimension=0,
            tiled=True,
        ),
        lax.psum_scatter(
            widen(grad_bias_value, model_width, part * width),
            ("dp", "tensor"),
            scatter_dimension=0,
            tiled=True,
        ),
        lax.psum_scatter(grad_bias_merge, ("dp", "tensor"), scatter_dimension=0, tiled=True),
        lax.psum_scatter(grad_gain_first, ("dp", "tensor"), scatter_dimension=0, tiled=True),
        lax.psum_scatter(grad_shift_first, ("dp", "tensor"), scatter_dimension=0, tiled=True),
        lax.psum_scatter(expand_bias_term, ("dp", "tensor"), scatter_dimension=0, tiled=True),
        lax.psum_scatter(grad_bias_shrink, ("dp", "tensor"), scatter_dimension=0, tiled=True),
        lax.psum_scatter(grad_gain_second, ("dp", "tensor"), scatter_dimension=0, tiled=True),
        lax.psum_scatter(grad_shift_second, ("dp", "tensor"), scatter_dimension=0, tiled=True),
    )
    querygrad, keygrad, valuegrad, mergegrad, expandgrad, shrinkgrad = (
        lax.psum_scatter(query_local, "dp", scatter_dimension=0, tiled=True),
        lax.psum_scatter(key_local, "dp", scatter_dimension=0, tiled=True),
        lax.psum_scatter(value_local, "dp", scatter_dimension=0, tiled=True),
        lax.psum_scatter(merge_local, "dp", scatter_dimension=1, tiled=True),
        lax.psum_scatter(expand_local, "dp", scatter_dimension=0, tiled=True),
        lax.psum_scatter(shrink_local, "dp", scatter_dimension=1, tiled=True),
    )
    return (
        output,
        tokens_grad,
        querygrad,
        qbiasgrad,
        keygrad,
        valuegrad,
        vbiasgrad,
        mergegrad,
        mbiasgrad,
        fgaingrad,
        fshiftgrad,
        expandgrad,
        ebiasgrad,
        shrinkgrad,
        sbiasgrad,
        sgaingrad,
        sshiftgrad,
    )


def solution(mesh):
    return jax.shard_map(
        on_device,
        mesh=mesh,
        in_specs=(
            P(("dp", "tensor"), None),
            P("dp", "tensor"),
            P("dp", "tensor"),
            P(("dp", "tensor")),
            P("dp", "tensor"),
            P("dp", "tensor"),
            P(("dp", "tensor")),
            P("tensor", "dp"),
            P(("dp", "tensor")),
            P(("dp", "tensor")),
            P(("dp", "tensor")),
            P("dp", "tensor"),
            P(("dp", "tensor")),
            P("tensor", "dp"),
            P(("dp", "tensor")),
            P(("dp", "tensor")),
            P(("dp", "tensor")),
            P(("dp", "tensor"), None),
        ),
        out_specs=(
            P(("dp", "tensor"), None),
            P(("dp", "tensor"), None),
            P("dp", "tensor"),
            P(("dp", "tensor")),
            P("dp", "tensor"),
            P("dp", "tensor"),
            P(("dp", "tensor")),
            P("tensor", "dp"),
            P(("dp", "tensor")),
            P(("dp", "tensor")),
            P(("dp", "tensor")),
            P("dp", "tensor"),
            P(("dp", "tensor")),
            P("tensor", "dp"),
            P(("dp", "tensor")),
            P(("dp", "tensor")),
            P(("dp", "tensor")),
        ),
        check_vma=False,
    )
```

profile of v0, /device:TPU:0, one launch (start us, length us, event | category | flops | bytes accessed | tf_op | source)
XLA Modules:
  0.0 1345.0 jit_solution(11370294428568450697)
XLA Ops:
  15.5 43.1 %all-reduce.19 = (f32[768]{0:T(1024)}, f32[768]{0:T(1024)}, f32[768]{0:T(1024)S(1)}, f32[768]{0:T(1024)S(1)}, f32[768]{0:T(1024)S(1)}, /*index=5*/f32[3072]{0:T(1024)}, f32[768]{0:T(1024)}, f32[768]{0:T(1024)}) all-reduce(f32[768]{0:T(1024)S(1)} %dynamic-update-slice.4, ...), channel_id=1, replica_groups=mesh['dp'=8,'tensor'=4] {'dp','tensor'}, use_global_device_ids=true, to_apply=%add.4 | all-reduce | flops 8448 | bytes 67584
  60.3 5.6 all_gather.60
  65.9 33.4 %all_gather.62 = bf16[768,192]{1,0:T(8,128)(2,1)} all-gather(bf16[96,192]{1,0:T(8,128)(2,1)} %param.24), channel_id=1, replica_groups=mesh['dp'=8,'tensor'=4] {'dp'}, dimensions={0}, use_global_device_ids=true | all-gather | bytes 331776 | tf_op jit(solution)/shard_map/all_gather | solution.py:143
  99.2 33.3 %all_gather.65 = bf16[768,192]{1,0:T(8,128)(2,1)} all-gather(bf16[96,192]{1,0:T(8,128)(2,1)} %param.27), channel_id=1, replica_groups=mesh['dp'=8,'tensor'=4] {'dp'}, dimensions={0}, use_global_device_ids=true | all-gather | bytes 331776 | tf_op jit(solution)/shard_map/all_gather | solution.py:145
  132.5 31.3 %all_gather.64 = bf16[768,192]{1,0:T(8,128)(2,1)S(1)} all-gather(bf16[96,192]{1,0:T(8,128)(2,1)} %param.26), channel_id=1, replica_groups=mesh['dp'=8,'tensor'=4] {'dp'}, dimensions={0}, use_global_device_ids=true | all-gather | bytes 331776 | tf_op jit(solution)/shard_map/all_gather | solution.py:144
  163.8 33.0 %all_gather.67 = bf16[192,768]{0,1:T(8,128)(2,1)} all-gather(bf16[192,96]{0,1:T(8,128)(2,1)S(1)} %copy.61), channel_id=1, replica_groups=mesh['dp'=8,'tensor'=4] {'dp'}, dimensions={1}, use_global_device_ids=true | all-gather | bytes 331776 | tf_op jit(solution)/shard_map/all_gather | solution.py:146
  197.7 4.2 fusion.30
  213.0 150.0 %while.32 = (s32[]{:T(128)}, bf16[12,512,64]{1,2,0:T(8,128)(2,1)}, f32[12,512]{1,0:T(8,128)}, s32[12]{0:T(128)S(1)}, s32[2048]{0:T(1024)S(1)}, /*index=5*/s32[1,...) while((s32[]{:T(128)}, bf16[12,512,64]{1,2,0:T(8,128)(2,1)}, ...), condition=%wide.region_3.4_spmd.clone, body=%wide.region_0.3_spmd.sunk.clone | while | flops 277872128 | bytes 33853836 | solution.py:61
  369.0 37.3 %reduce-scatter.19.cloned.1.call-done = bf16[512,768]{1,0:T(8,128)(2,1)} async-done(((bf16[2048,768]{1,0:T(8,128)(2,1)}), bf16[512,768]{1,0:T(8,128)(2,1)}) %reduce-scatter.19.cloned.1.call-update) | async-done | bytes 786448 | tf_op jit(solution)/shard_map/reduce_scatter | solution.py:192
  412.4 29.0 %all-gather.9.cloned.1.call-done = bf16[2048,768]{1,0:T(8,128)(2,1)} async-done(((bf16[512,768]{1,0:T(8,128)(2,1)}), bf16[2048,768]{1,0:T(8,128)(2,1)}) %all-gather.9.cloned.1.call-update) | async-done | bytes 3145744 | tf_op jit(solution)/shard_map/all_gather | solution.py:200
  441.3 19.0 %multiply_convert_fusion.1 = (bf16[2048,768]{1,0:T(8,128)(2,1)}, f32[2048,768]{1,0:T(8,128)}, f32[2048,768]{1,0:T(8,128)}) fusion(f32[768]{0:T(1024)S(1)} %dynamic_slice.96, bf16[2048,768]{1,0:T(8,128)(2,1)} %all-gather.9.cloned.1.call-done, bf16[768,768]{1,0:T(8,128)(2,1)} %all-gather.11.cloned.1.call-done), kind=kOutput, calls=%fused_computation.39 | convolution fusion | flops 2519728128 | bytes 20057088 | tf_op jit(solution)/shard_map/dot_general | solution.py:202
  460.3 24.9 %all-gather.13.cloned.1.call-done = bf16[768,768]{0,1:T(8,128)(2,1)} async-done(((bf16[768,96]{0,1:T(8,128)(2,1)}), bf16[768,768]{0,1:T(8,128)(2,1)}) %all-gather.13.cloned.1.call-update) | async-done | bytes 1179664 | tf_op jit(solution)/shard_map/all_gather | solution.py:148
  485.2 6.5 convolution_convert_fusion.1
  491.8 36.3 %reduce-scatter.21.cloned.1.call-done = bf16[512,768]{1,0:T(8,128)(2,1)} async-done(((bf16[2048,768]{1,0:T(8,128)(2,1)}), bf16[512,768]{1,0:T(8,128)(2,1)}) %reduce-scatter.21.cloned.1.call-update) | async-done | bytes 786448 | tf_op jit(solution)/shard_map/reduce_scatter | solution.py:207
  534.3 28.4 %all-gather.15.cloned.1.call-done = bf16[2048,768]{1,0:T(8,128)(2,1)} async-done(((bf16[512,768]{1,0:T(8,128)(2,1)}), bf16[2048,768]{1,0:T(8,128)(2,1)}) %all-gather.15.cloned.1.call-update) | async-done | bytes 3145744 | tf_op jit(solution)/shard_map/all_gather | solution.py:219
  562.8 11.1 fusion.50
  575.5 4.1 convolution_convert_fusion
  579.7 37.9 %reduce-scatter.23.cloned.1.call-done = bf16[512,768]{1,0:T(8,128)(2,1)} async-done(((bf16[2048,768]{1,0:T(8,128)(2,1)}), bf16[512,768]{1,0:T(8,128)(2,1)}) %reduce-scatter.23.cloned.1.call-update) | async-done | bytes 786448 | tf_op jit(solution)/shard_map/reduce_scatter | solution.py:234
  625.6 28.2 %all-gather.17.cloned.1.call-done = bf16[2048,768]{1,0:T(8,128)(2,1)} async-done(((bf16[512,768]{1,0:T(8,128)(2,1)}), bf16[2048,768]{1,0:T(8,128)(2,1)}) %all-gather.17.cloned.1.call-update) | async-done | bytes 3145744 | tf_op jit(solution)/shard_map/all_gather | solution.py:246
  658.1 228.1 %while.33 = (s32[]{:T(128)}, f32[2048,192]{0,1:T(8,128)S(1)}, f32[2048,192]{0,1:T(8,128)S(1)}, f32[12,512,64]{1,2,0:T(8,128)}, s32[12]{0:T(128)S(1)}, /*index=5*...) while((s32[]{:T(128)}, f32[2048,192]{0,1:T(8,128)S(1)}, ...), condition=%wide.region_17.18_spmd.clone, body=%wide.region_15.17_spmd.sunk.clone | while | flops 682884608 | bytes 55606196 | solution.py:111
  743.4 4.0 multiply_reduce_fusion.7
  857.4 4.0 multiply_reduce_fusion.7
  898.6 7.0 fusion.57
  905.6 6.9 fusion.36
  932.4 22.5 %reduce-scatter.37.cloned.1.call-done = f32[96,192]{1,0:T(8,128)} async-done(((f32[768,192]{1,0:T(8,128)}), f32[96,192]{1,0:T(8,128)}) %reduce-scatter.37.cloned.1.call-update) | async-done | bytes 73744
  956.6 37.7 %reduce-scatter.25.cloned.1.call-done = bf16[512,768]{1,0:T(8,128)(2,1)} async-done(((bf16[2048,768]{1,0:T(8,128)(2,1)}), bf16[512,768]{1,0:T(8,128)(2,1)}) %reduce-scatter.25.cloned.1.call-update) | async-done | bytes 786448 | tf_op jit(solution)/shard_map/reduce_scatter | solution.py:278
  997.1 41.4 %all-reduce.18 = (f32[768]{0:T(1024)S(1)}, f32[768]{0:T(1024)S(1)}, f32[768]{0:T(1024)S(1)}, f32[768]{0:T(1024)S(1)}, f32[768]{0:T(1024)S(1)}, /*index=5*/f32[76...) all-reduce(f32[768]{0:T(1024)S(1)} %dynamic-update-slice.8, ...), channel_id=1, replica_groups=mesh['dp'=8,'tensor'=4] {'dp','tensor'}, use_global_device_ids=true, to_apply=%add.8 | all-reduce | flops 9984 | bytes 79872
  1045.0 22.9 %reduce-scatter.29.cloned.1.call-done = f32[768,96]{0,1:T(8,128)} async-done(((f32[768,768]{0,1:T(8,128)}), f32[768,96]{0,1:T(8,128)}) %reduce-scatter.29.cloned.1.call-update) | async-done | bytes 294928 | tf_op jit(solution)/shard_map/reduce_scatter | solution.py:327
  1068.0 72.4 %reduce-scatter.27.cloned.1.call-done = f32[96,768]{1,0:T(8,128)} async-done(((f32[768,768]{1,0:T(8,128)}), f32[96,768]{1,0:T(8,128)}) %reduce-scatter.27.cloned.1.call-update) | async-done | bytes 294928 | tf_op jit(solution)/shard_map/reduce_scatter | solution.py:326
  1140.3 66.0 %reduce-scatter.31.cloned.1.call-done = f32[96,192]{1,0:T(8,128)} async-done(((f32[768,192]{1,0:T(8,128)}), f32[96,192]{1,0:T(8,128)}) %reduce-scatter.31.cloned.1.call-update) | async-done | bytes 73744
  1206.3 65.4 %reduce-scatter.33.cloned.1.call-done = f32[96,192]{1,0:T(8,128)} async-done(((f32[768,192]{1,0:T(8,128)}), f32[96,192]{1,0:T(8,128)}) %reduce-scatter.33.cloned.1.call-update) | async-done | bytes 73744
  1271.8 65.9 %reduce-scatter.35.cloned.1.call-done = f32[96,192]{1,0:T(8,128)} async-done(((f32[768,192]{1,0:T(8,128)}), f32[96,192]{1,0:T(8,128)}) %reduce-scatter.35.cloned.1.call-update) | async-done | bytes 73744
  (494 shorter events, 394.5 us)
Async XLA Ops:
  8.0 189.7 %all-gather.7.cloned.1.call-start = ((), (), s32[]{:S(2)}) async-start(), calls=%async_computation.10 | async-start | bytes 3932160 | tf_op jit(solution)/shard_map/all_gather | solution.py:179
  8.8 397.5 %reduce-scatter.19.cloned.1.call-start = ((), (), s32[]{:S(2)}) async-start(), calls=%async_computation.11 | async-start | bytes 3932160 | tf_op jit(solution)/shard_map/reduce_scatter | solution.py:192
  163.8 45.6 %copy-start.11 = (bf16[768,192]{1,0:T(8,128)(2,1)}, bf16[768,192]{1,0:T(8,128)(2,1)S(1)}, u32[]{:S(2)}) copy-start(bf16[768,192]{1,0:T(8,128)(2,1)S(1)} %all_gather.64) | copy-start | bytes 884740
  365.4 40.9 %copy-start.5 = (bf16[512,768]{1,0:T(8,128)(2,1)S(1)}, bf16[512,768]{1,0:T(8,128)(2,1)}, u32[]{:S(2)}) copy-start(bf16[512,768]{1,0:T(8,128)(2,1)} %param.22) | copy-start | bytes 2359300
  368.1 41.3 %copy-start.22 = (f32[768]{0:T(1024)S(1)}, f32[768]{0:T(1024)}, u32[]{:S(2)}) copy-start(f32[768]{0:T(1024)} %get-tuple-element.467) | copy-start | bytes 9220
  368.1 41.3 %copy-start.39 = (f32[768]{0:T(1024)S(1)}, f32[768]{0:T(1024)}, u32[]{:S(2)}) copy-start(f32[768]{0:T(1024)} %get-tuple-element.466) | copy-start | bytes 9220
  368.2 44.2 %all-gather.11.cloned.1.call-start = ((), (), s32[]{:S(2)}) async-start(), calls=%async_computation.13 | async-start | bytes 1327104 | tf_op jit(solution)/shard_map/all_gather | solution.py:147
  368.8 72.6 %all-gather.9.cloned.1.call-start = ((), (), s32[]{:S(2)}) async-start(), calls=%async_computation.12 | async-start | bytes 3932160 | tf_op jit(solution)/shard_map/all_gather | solution.py:200
  409.4 50.9 %copy-start.33 = (f32[512]{0:T(512)}, f32[512]{0:T(512)S(1)}, u32[]{:S(2)}) copy-start(f32[512]{0:T(512)S(1)} %multiply_reduce_fusion.4) | copy-start | bytes 6148
  409.4 118.7 %copy-start.24 = (f32[512]{0:T(512)}, f32[512]{0:T(512)S(1)}, u32[]{:S(2)}) copy-start(f32[512]{0:T(512)S(1)} %fusion.47) | copy-start | bytes 6148
  410.8 74.3 %all-gather.13.cloned.1.call-start = ((), (), s32[]{:S(2)}) async-start(), calls=%async_computation.14 | async-start | bytes 1327104 | tf_op jit(solution)/shard_map/all_gather | solution.py:148
  411.4 116.7 %reduce-scatter.21.cloned.1.call-start = ((), (), s32[]{:S(2)}) async-start(), calls=%async_computation.15 | async-start | bytes 3932160 | tf_op jit(solution)/shard_map/reduce_scatter | solution.py:207
  412.3 48.0 %copy-start.41 = (f32[768]{0:T(1024)}, f32[768]{0:T(1024)S(1)}, u32[]{:S(2)}) copy-start(f32[768]{0:T(1024)S(1)} %dynamic_slice.96) | copy-start | bytes 9220
  491.7 71.0 %all-gather.15.cloned.1.call-start = ((), (), s32[]{:S(2)}) async-start(), calls=%async_computation.16 | async-start | bytes 3932160 | tf_op jit(solution)/shard_map/all_gather | solution.py:219
  534.1 83.5 %reduce-scatter.23.cloned.1.call-start = ((), (), s32[]{:S(2)}) async-start(), calls=%async_computation.17 | async-start | bytes 3932160 | tf_op jit(solution)/shard_map/reduce_scatter | solution.py:234
  579.7 74.1 %all-gather.17.cloned.1.call-start = ((), (), s32[]{:S(2)}) async-start(), calls=%async_computation.18 | async-start | bytes 3932160 | tf_op jit(solution)/shard_map/all_gather | solution.py:246
  625.1 329.8 %reduce-scatter.37.cloned.1.call-start = ((), (), s32[]{:S(2)}) async-start(), calls=%async_computation.25 | async-start | bytes 884736
  892.2 102.1 %reduce-scatter.25.cloned.1.call-start = ((), (), s32[]{:S(2)}) async-start(), calls=%async_computation.19 | async-start | bytes 3932160 | tf_op jit(solution)/shard_map/reduce_scatter | solution.py:278
  898.4 169.6 %reduce-scatter.29.cloned.1.call-start = ((), (), s32[]{:S(2)}) async-start(), calls=%async_computation.21 | async-start | bytes 2654208 | tf_op jit(solution)/shard_map/reduce_scatter | solution.py:327
  905.6 234.8 %reduce-scatter.27.cloned.1.call-start = ((), (), s32[]{:S(2)}) async-start(), calls=%async_computation.20 | async-start | bytes 2654208 | tf_op jit(solution)/shard_map/reduce_scatter | solution.py:326
  912.6 293.8 %reduce-scatter.31.cloned.1.call-start = ((), (), s32[]{:S(2)}) async-start(), calls=%async_computation.22 | async-start | bytes 884736
  918.7 353.1 %reduce-scatter.33.cloned.1.call-start = ((), (), s32[]{:S(2)}) async-start(), calls=%async_computation.23 | async-start | bytes 884736
  924.5 413.2 %reduce-scatter.35.cloned.1.call-start = ((), (), s32[]{:S(2)}) async-start(), calls=%async_computation.24 | async-start | bytes 884736
  929.0 68.1 %copy-start.34 = (f32[768]{0:T(1024)S(1)}, f32[768]{0:T(1024)}, u32[]{:S(2)}) copy-start(f32[768]{0:T(1024)} %get-tuple-element.409) | copy-start | bytes 9220
  929.0 68.1 %copy-start.35 = (f32[768]{0:T(1024)S(1)}, f32[768]{0:T(1024)}, u32[]{:S(2)}) copy-start(f32[768]{0:T(1024)} %get-tuple-element.413) | copy-start | bytes 9220
  929.0 68.1 %copy-start.36 = (f32[768]{0:T(1024)S(1)}, f32[768]{0:T(1024)}, u32[]{:S(2)}) copy-start(f32[768]{0:T(1024)} %get-tuple-element.407) | copy-start | bytes 9220
  929.0 68.1 %copy-start.37 = (f32[768]{0:T(1024)S(1)}, f32[768]{0:T(1024)}, u32[]{:S(2)}) copy-start(f32[768]{0:T(1024)} %get-tuple-element.411) | copy-start | bytes 9220
  929.0 68.1 %copy-start.38 = (f32[768]{0:T(1024)S(1)}, f32[768]{0:T(1024)}, u32[]{:S(2)}) copy-start(f32[768]{0:T(1024)} %get-tuple-element.412) | copy-start | bytes 9220
  929.0 114.8 %copy-start.4 = (f32[512,768]{1,0:T(8,128)S(1)}, f32[512,768]{1,0:T(8,128)}, u32[]{:S(2)}) copy-start(f32[512,768]{1,0:T(8,128)} %copy-done.3) | copy-start | bytes 4718596
  929.0 114.8 %copy-start.26 = (f32[512]{0:T(512)S(1)}, f32[512]{0:T(512)}, u32[]{:S(2)}) copy-start(f32[512]{0:T(512)} %copy-done.25) | copy-start | bytes 6148
  929.0 114.8 %copy-start.29 = (f32[768]{0:T(1024)S(1)}, f32[768]{0:T(1024)}, u32[]{:S(2)}) copy-start(f32[768]{0:T(1024)} %get-tuple-element.473) | copy-start | bytes 9220
  929.0 114.8 %copy-start.32 = (f32[512]{0:T(512)S(1)}, f32[512]{0:T(512)}, u32[]{:S(2)}) copy-start(f32[512]{0:T(512)} %copy-done.31) | copy-start | bytes 6148
  (74 other events, 326.5 us)
Sparse Core Ops, SparseCore 0:
  10.4 31.9 all-gather.6
  368.3 37.9 reduce-scatter.18
  534.2 28.5 all-gather.14
  625.2 28.5 all-gather.16
Sparse Core Ops, SparseCore 1:
  370.8 41.5 all-gather.10
  414.5 26.8 all-gather.8
  443.6 41.5 all-gather.12
  491.8 36.3 reduce-scatter.20
  579.7 37.8 reduce-scatter.22
  892.3 62.6 reduce-scatter.36
  957.3 36.9 reduce-scatter.24
  998.6 69.3 reduce-scatter.28
  1072.3 68.0 reduce-scatter.26
  1144.6 61.7 reduce-scatter.30
  1210.1 61.6 reduce-scatter.32
  1276.0 61.6 reduce-scatter.34
where the time goes:
time: 1360 us; the launch traced here: 1340 us
  waiting for transfers between devices  577 us (42%)
  matrix products  307 us (23%)
  blocking collectives  221 us (16%)
  local copies, waits for them, and re-layouts  112 us (8%)
  loops' own time  71.6 us (5%)
  other arithmetic  38.9 us (3%)
  between operations  16.2 us (1%)
    unnamed x20, waiting for transfers between devices  222 us
    unnamed x2, blocking collectives  84.6 us
    reduce_scatter x1, waiting for transfers between devices, on_device(): lax.psum_scatter(expand_local, 'dp', scatter_dimension=0, tiled=True)  72.4 us
    dot_general x24, matrix products, one(): lax.dot_general(query_rows, key_head, CONTRACT_COLUMNS, preferred_element...  70.4 us
    another operation x1, loops' own time, attend_back(): lax.scan(one, (empty, empty), jnp.arange(count * heads))  47.7 us
    dot_general x12, matrix products, one(): lax.dot_general(grad_rows, value_head, CONTRACT_COLUMNS, preferred_elemen...  47.1 us
    dot_general x12, matrix products, one(): context = jnp.dot(chance, value_head, preferred_element_type=jnp.float32)  46.9 us
    reduce_scatter x1, waiting for transfers between devices, on_device(): lax.psum_scatter(lax.dot_general(inner_low, expand_full, CONTRACT_COLUMNS...  37.9 us
  transfers between devices with their start and end apart: 16, of which 15 were waited for; matrix products, arithmetic and copies ran while one was open for 6% of the time, Pallas kernels for 0%

commit v1 on v0

--- a/solution.py
+++ b/solution.py
@@ -1,3 +1,4 @@
+import functools
 import jax
 import jax.numpy as jnp
 from jax import lax
@@ -7,6 +8,26 @@
 EPSILON = 1e-12
 CONTRACT_ROWS = (((0,), (0,)), ((), ()))
 CONTRACT_COLUMNS = (((1,), (1,)), ((), ()))
+
+
+def spread_shapes_by_axis(raw, along_axis):
+    aux = lax.axis_size(along_axis)
+    tmp, everything = (aux, lax.axis_index(along_axis))
+    all_values, piece_now = (raw, 1)
+    while piece_now < tmp:
+        lower = lax.ppermute(
+            all_values,
+            axis_name=along_axis,
+            perm=list(map(lambda j0: (j0, j0 ^ piece_now), range(tmp))),
+        )
+        z_new = jnp.concatenate([all_values, lower], axis=0)
+        later = jnp.concatenate([lower, all_values], axis=0)
+        all_values = jnp.where(everything & piece_now == 0, z_new, later)
+        piece_now = 2 * piece_now
+    return all_values
+
+
+enter_gates_by_axis = functools.partial(spread_shapes_by_axis, along_axis="tensor")
 
 
 def normalize(values, gain, shift):
@@ -197,7 +218,7 @@
     ).astype(jnp.float32)
     mixed = tokens.astype(jnp.float32) + attended + bias_merge
     hidden = normalize(mixed, gain_first, shift_first)
-    full_hidden = lax.all_gather(hidden.astype(jnp.bfloat16), "tensor", axis=0, tiled=True)
+    full_hidden = enter_gates_by_axis(hidden.astype(jnp.bfloat16))
     inner = (
         jnp.dot(full_hidden, expand_full, preferred_element_type=jnp.float32) + local_expand_bias
     )

time: 1360 us -> 1270 us (0.934)
  matrix products: 307 us -> 238 us
  local copies, waits for them, and re-layouts: 112 us -> 87.1 us
    all_gather x1, waiting for transfers between devices: 0.12 us -> 36.3 us  [on_device(): lax.all_gather(expand_proj, 'dp', axis=0, tiled=True)]
    all_gather x1 -> x0, waiting for transfers between devices: 29 us -> none  [on_device(): lax.all_gather(hidden.astype(jnp.bfloat16), 'tensor', axis=0, tiled=True)]
    while x96 -> x48, local copies, waits for them, and re-layouts: 32.7 us -> 6.31 us
    dot_general x12, matrix products: 46.9 us -> 21.7 us  [one(): context = jnp.dot(chance, value_head, preferred_element_type=jnp.float32)]
    dot_general x12, matrix products: 47.1 us -> 22.6 us  [one(): lax.dot_general(grad_rows, value_head, CONTRACT_COLUMNS, preferred_elemen...]
    dot_general x24, matrix products: 70.4 us -> 51.9 us  [one(): lax.dot_general(query_rows, key_head, CONTRACT_COLUMNS, preferred_element...]
    unnamed x20 -> x19, waiting for transfers between devices: 222 us -> 216 us
  transfers between devices with their start and end apart: 16 -> 17, of which waited for: 15 -> 15; matrix products, arithmetic and copies ran while one was open for 6% -> 7% of each run, Pallas kernels for 0% -> 0%
where the time goes in v1:
time: 1270 us; the launch traced here: 1260 us
  waiting for transfers between devices  578 us (46%)
  matrix products  238 us (19%)
  blocking collectives  222 us (17%)
  local copies, waits for them, and re-layouts  87.1 us (7%)
  loops' own time  71.4 us (6%)
  other arithmetic  46.8 us (4%)
  between operations  16.7 us (1%)
    unnamed x19, waiting for transfers between devices  216 us
    unnamed x2, blocking collectives  84.8 us
    reduce_scatter x1, waiting for transfers between devices, on_device(): lax.psum_scatter(expand_local, 'dp', scatter_dimension=0, tiled=True)  72.7 us
    dot_general x24, matrix products, one(): lax.dot_general(query_rows, key_head, CONTRACT_COLUMNS, preferred_element...  51.9 us
    another operation x1, loops' own time, attend_back(): lax.scan(one, (empty, empty), jnp.arange(count * heads))  47.5 us
    reduce_scatter x1, waiting for transfers between devices, on_device(): lax.psum_scatter(lax.dot_general(inner_low, expand_full, CONTRACT_COLUMNS...  38.1 us
    reduce_scatter x1, waiting for transfers between devices, on_device(): lax.psum_scatter((total + lax.dot_general(value_low, value_full, CONTRACT...  37.8 us
    reduce_scatter x1, waiting for transfers between devices, on_device(): lax.psum_scatter(jnp.dot(context_low, merge_full, preferred_element_type=...  37.8 us
  transfers between devices with their start and end apart: 17, of which 15 were waited for; matrix products, arithmetic and copies ran while one was open for 7% of the time, Pallas kernels for 0%

profile of v1, /device:TPU:0, one launch (start us, length us, event | category | flops | bytes accessed | tf_op | source)
XLA Modules:
  0.0 1261.2 jit_solution(12784737073061207752)
XLA Ops:
  15.5 43.1 %all-reduce.19 = (f32[768]{0:T(1024)}, f32[768]{0:T(1024)}, f32[768]{0:T(1024)S(1)}, f32[768]{0:T(1024)S(1)}, f32[768]{0:T(1024)S(1)}, /*index=5*/f32[3072]{0:T(1024)}, f32[768]{0:T(1024)}, f32[768]{0:T(1024)}) all-reduce(f32[768]{0:T(1024)S(1)} %dynamic-update-slice.4, ...), channel_id=1, replica_groups=mesh['dp'=8,'tensor'=4] {'dp','tensor'}, use_global_device_ids=true, to_apply=%add.4 | all-reduce | flops 8448 | bytes 67584
  60.3 5.6 all_gather.57
  65.9 33.2 %all_gather.64 = bf16[192,768]{0,1:T(8,128)(2,1)} all-gather(bf16[192,96]{0,1:T(8,128)(2,1)S(1)} %copy.61), channel_id=1, replica_groups=mesh['dp'=8,'tensor'=4] {'dp'}, dimensions={1}, use_global_device_ids=true | all-gather | bytes 331776 | tf_op jit(solution)/shard_map/all_gather | solution.py:167
  99.0 33.3 %all_gather.59 = bf16[768,192]{1,0:T(8,128)(2,1)} all-gather(bf16[96,192]{1,0:T(8,128)(2,1)} %param.24), channel_id=1, replica_groups=mesh['dp'=8,'tensor'=4] {'dp'}, dimensions={0}, use_global_device_ids=true | all-gather | bytes 331776 | tf_op jit(solution)/shard_map/all_gather | solution.py:164
  132.3 31.5 %all_gather.61 = bf16[768,192]{1,0:T(8,128)(2,1)S(1)} all-gather(bf16[96,192]{1,0:T(8,128)(2,1)} %param.26), channel_id=1, replica_groups=mesh['dp'=8,'tensor'=4] {'dp'}, dimensions={0}, use_global_device_ids=true | all-gather | bytes 331776 | tf_op jit(solution)/shard_map/all_gather | solution.py:165
  163.8 33.2 %all_gather.62 = bf16[768,192]{1,0:T(8,128)(2,1)} all-gather(bf16[96,192]{1,0:T(8,128)(2,1)} %param.27), channel_id=1, replica_groups=mesh['dp'=8,'tensor'=4] {'dp'}, dimensions={0}, use_global_device_ids=true | all-gather | bytes 331776 | tf_op jit(solution)/shard_map/all_gather | solution.py:166
  197.9 4.2 fusion.31
  213.2 106.4 %while.32 = (s32[]{:T(128)}, bf16[12,512,64]{1,2,0:T(8,128)(2,1)}, f32[12,512]{1,0:T(8,128)}, s32[12]{0:T(128)S(1)}, s32[2048]{0:T(1024)S(1)}, /*index=5*/s32[1,...) while((s32[]{:T(128)}, bf16[12,512,64]{1,2,0:T(8,128)(2,1)}, ...), condition=%wide.region_3.4_spmd.clone, body=%wide.region_0.3_spmd.sunk.clone | while | flops 277872128 | bytes 17076092 | solution.py:82
  325.0 37.8 %reduce-scatter.19.cloned.1.call-done = bf16[512,768]{1,0:T(8,128)(2,1)} async-done(((bf16[2048,768]{1,0:T(8,128)(2,1)}), bf16[512,768]{1,0:T(8,128)(2,1)}) %reduce-scatter.19.cloned.1.call-update) | async-done | bytes 786448 | tf_op jit(solution)/shard_map/reduce_scatter | solution.py:213
  372.4 36.3 %all-gather.8.cloned.1.call-done = bf16[768,768]{1,0:T(8,128)(2,1)} async-done(((bf16[96,768]{1,0:T(8,128)(2,1)}), bf16[768,768]{1,0:T(8,128)(2,1)}) %all-gather.8.cloned.1.call-update) | async-done | bytes 1179664 | tf_op jit(solution)/shard_map/all_gather | solution.py:168
  408.6 21.0 %multiply_convert_fusion.1 = (bf16[2048,768]{1,0:T(8,128)(2,1)}, f32[2048,768]{1,0:T(8,128)}, f32[2048,768]{1,0:T(8,128)}) fusion(f32[768]{0:T(1024)S(1)} %dynamic_slice.96, bf16[768,768]{1,0:T(8,128)(2,1)} %all-gather.8.cloned.1.call-done, bf16[1024,768]{1,0:T(8,128)(2,1)} %collective-permute-done.1, bf16[1024,768]{1,0:T(8,128)(2,1)} %maximum_select_fusion.1, ...), kind=kOutput, calls=%fused_computation.39 | convolution fusion | flops 2533883904 | bytes 20057088 | tf_op jit(solution)/shard_map/dot_general | solution.py:223
  429.6 21.3 %all-gather.10.cloned.1.call-done = bf16[768,768]{0,1:T(8,128)(2,1)} async-done(((bf16[768,96]{0,1:T(8,128)(2,1)}), bf16[768,768]{0,1:T(8,128)(2,1)}) %all-gather.10.cloned.1.call-update) | async-done | bytes 1179664 | tf_op jit(solution)/shard_map/all_gather | solution.py:169
  450.9 6.5 convolution_convert_fusion.1
  457.6 36.5 %reduce-scatter.21.cloned.1.call-done = bf16[512,768]{1,0:T(8,128)(2,1)} async-done(((bf16[2048,768]{1,0:T(8,128)(2,1)}), bf16[512,768]{1,0:T(8,128)(2,1)}) %reduce-scatter.21.cloned.1.call-update) | async-done | bytes 786448 | tf_op jit(solution)/shard_map/reduce_scatter | solution.py:228
  500.4 28.4 %all-gather.12.cloned.1.call-done = bf16[2048,768]{1,0:T(8,128)(2,1)} async-done(((bf16[512,768]{1,0:T(8,128)(2,1)}), bf16[2048,768]{1,0:T(8,128)(2,1)}) %all-gather.12.cloned.1.call-update) | async-done | bytes 3145744 | tf_op jit(solution)/shard_map/all_gather | solution.py:240
  528.8 5.0 fusion.59
  533.8 6.9 fusion.53
  542.3 4.0 convolution_convert_fusion
  546.4 38.1 %reduce-scatter.23.cloned.1.call-done = bf16[512,768]{1,0:T(8,128)(2,1)} async-done(((bf16[2048,768]{1,0:T(8,128)(2,1)}), bf16[512,768]{1,0:T(8,128)(2,1)}) %reduce-scatter.23.cloned.1.call-update) | async-done | bytes 786448 | tf_op jit(solution)/shard_map/reduce_scatter | solution.py:255
  592.4 28.2 %all-gather.14.cloned.1.call-done = bf16[2048,768]{1,0:T(8,128)(2,1)} async-done(((bf16[512,768]{1,0:T(8,128)(2,1)}), bf16[2048,768]{1,0:T(8,128)(2,1)}) %all-gather.14.cloned.1.call-update) | async-done | bytes 3145744 | tf_op jit(solution)/shard_map/all_gather | solution.py:267
  625.0 178.2 %while.33 = (s32[]{:T(128)}, f32[2048,192]{0,1:T(8,128)S(1)}, f32[2048,192]{0,1:T(8,128)S(1)}, f32[12,512,64]{1,2,0:T(8,128)}, s32[12]{0:T(128)S(1)}, /*index=5*...) while((s32[]{:T(128)}, f32[2048,192]{0,1:T(8,128)S(1)}, ...), condition=%wide.region_17.18_spmd.clone, body=%wide.region_15.17_spmd.sunk.clone | while | flops 682884608 | bytes 38828452 | solution.py:132
  803.2 4.4 convolution_bitcast_fusion.1
  815.7 7.0 fusion.61
  822.8 8.0 fusion.36
  852.5 17.8 %reduce-scatter.37.cloned.1.call-done = f32[96,192]{1,0:T(8,128)} async-done(((f32[768,192]{1,0:T(8,128)}), f32[96,192]{1,0:T(8,128)}) %reduce-scatter.37.cloned.1.call-update) | async-done | bytes 73744
  871.9 37.8 %reduce-scatter.25.cloned.1.call-done = bf16[512,768]{1,0:T(8,128)(2,1)} async-done(((bf16[2048,768]{1,0:T(8,128)(2,1)}), bf16[512,768]{1,0:T(8,128)(2,1)}) %reduce-scatter.25.cloned.1.call-update) | async-done | bytes 786448 | tf_op jit(solution)/shard_map/reduce_scatter | solution.py:299
  912.5 41.7 %all-reduce.18 = (f32[768]{0:T(1024)S(1)}, f32[768]{0:T(1024)S(1)}, f32[768]{0:T(1024)S(1)}, f32[768]{0:T(1024)S(1)}, f32[768]{0:T(1024)S(1)}, /*index=5*/f32[76...) all-reduce(f32[768]{0:T(1024)S(1)} %dynamic-update-slice.8, ...), channel_id=1, replica_groups=mesh['dp'=8,'tensor'=4] {'dp','tensor'}, use_global_device_ids=true, to_apply=%add.8 | all-reduce | flops 9984 | bytes 79872
  960.7 23.2 %reduce-scatter.29.cloned.1.call-done = f32[768,96]{0,1:T(8,128)} async-done(((f32[768,768]{0,1:T(8,128)}), f32[768,96]{0,1:T(8,128)}) %reduce-scatter.29.cloned.1.call-update) | async-done | bytes 294928 | tf_op jit(solution)/shard_map/reduce_scatter | solution.py:348
  983.8 72.7 %reduce-scatter.27.cloned.1.call-done = f32[96,768]{1,0:T(8,128)} async-done(((f32[768,768]{1,0:T(8,128)}), f32[96,768]{1,0:T(8,128)}) %reduce-scatter.27.cloned.1.call-update) | async-done | bytes 294928 | tf_op jit(solution)/shard_map/reduce_scatter | solution.py:347
  1056.5 65.8 %reduce-scatter.31.cloned.1.call-done = f32[96,192]{1,0:T(8,128)} async-done(((f32[768,192]{1,0:T(8,128)}), f32[96,192]{1,0:T(8,128)}) %reduce-scatter.31.cloned.1.call-update) | async-done | bytes 73744
  1122.3 65.4 %reduce-scatter.35.cloned.1.call-done = f32[96,192]{1,0:T(8,128)} async-done(((f32[768,192]{1,0:T(8,128)}), f32[96,192]{1,0:T(8,128)}) %reduce-scatter.35.cloned.1.call-update) | async-done | bytes 73744
  1187.7 65.7 %reduce-scatter.33.cloned.1.call-done = f32[96,192]{1,0:T(8,128)} async-done(((f32[768,192]{1,0:T(8,128)}), f32[96,192]{1,0:T(8,128)}) %reduce-scatter.33.cloned.1.call-update) | async-done | bytes 73744
  (455 shorter events, 309.8 us)
Async XLA Ops:
  8.0 189.9 %all-gather.6.cloned.1.call-start = ((), (), s32[]{:S(2)}) async-start(), calls=%async_computation.10 | async-start | bytes 3932160 | tf_op jit(solution)/shard_map/all_gather | solution.py:200
  8.8 354.0 %reduce-scatter.19.cloned.1.call-start = ((), (), s32[]{:S(2)}) async-start(), calls=%async_computation.11 | async-start | bytes 3932160 | tf_op jit(solution)/shard_map/reduce_scatter | solution.py:213
  163.8 45.9 %copy-start.10 = (bf16[768,192]{1,0:T(8,128)(2,1)}, bf16[768,192]{1,0:T(8,128)(2,1)S(1)}, u32[]{:S(2)}) copy-start(bf16[768,192]{1,0:T(8,128)(2,1)S(1)} %all_gather.61) | copy-start | bytes 884740
  322.0 40.7 %copy-start.3 = (bf16[512,768]{1,0:T(8,128)(2,1)S(1)}, bf16[512,768]{1,0:T(8,128)(2,1)}, u32[]{:S(2)}) copy-start(bf16[512,768]{1,0:T(8,128)(2,1)} %param.22) | copy-start | bytes 2359300
  324.7 41.8 %copy-start.20 = (f32[768]{0:T(1024)S(1)}, f32[768]{0:T(1024)}, u32[]{:S(2)}) copy-start(f32[768]{0:T(1024)} %get-tuple-element.467) | copy-start | bytes 9220
  324.7 41.8 %copy-start.42 = (f32[768]{0:T(1024)S(1)}, f32[768]{0:T(1024)}, u32[]{:S(2)}) copy-start(f32[768]{0:T(1024)} %get-tuple-element.466) | copy-start | bytes 9220
  324.8 83.8 %all-gather.8.cloned.1.call-start = ((), (), s32[]{:S(2)}) async-start(), calls=%async_computation.12 | async-start | bytes 1327104 | tf_op jit(solution)/shard_map/all_gather | solution.py:168
  367.0 2.4 collective-permute-start
  367.1 83.9 %all-gather.10.cloned.1.call-start = ((), (), s32[]{:S(2)}) async-start(), calls=%async_computation.13 | async-start | bytes 1327104 | tf_op jit(solution)/shard_map/all_gather | solution.py:169
  371.2 37.4 %collective-permute-start.1 = (bf16[1024,768]{1,0:T(8,128)(2,1)}, bf16[1024,768]{1,0:T(8,128)(2,1)}, u32[]{:S(2)}, u32[]{:S(2)}) collective-permute-start(bf16[1024,768]{1,0:T(8,128)(2,1)} %maximum_select_fusion.1), channel_id=1, source_target_pairs={{0,2},{1,3},{2,0},{3,1},{4,6},{5,7},{6,4},{7,5},{8,10},{9,11},{10,... | collective-permute-start | bytes 4718600 | tf_op jit(solution)/shard_map/ppermute | solution.py:18
  371.5 122.6 %reduce-scatter.21.cloned.1.call-start = ((), (), s32[]{:S(2)}) async-start(), calls=%async_computation.14 | async-start | bytes 3932160 | tf_op jit(solution)/shard_map/reduce_scatter | solution.py:228
  372.4 57.3 %copy-start.40 = (f32[768]{0:T(1024)}, f32[768]{0:T(1024)S(1)}, u32[]{:S(2)}) copy-start(f32[768]{0:T(1024)S(1)} %dynamic_slice.96) | copy-start | bytes 9220
  457.5 39.0 %copy-start.15 = (bf16[512,768]{1,0:T(8,128)(2,1)S(1)}, bf16[512,768]{1,0:T(8,128)(2,1)}, u32[]{:S(2)}) copy-start(bf16[512,768]{1,0:T(8,128)(2,1)} %param.39) | copy-start | bytes 2359300
  457.6 71.2 %all-gather.12.cloned.1.call-start = ((), (), s32[]{:S(2)}) async-start(), calls=%async_computation.15 | async-start | bytes 3932160 | tf_op jit(solution)/shard_map/all_gather | solution.py:240
  500.1 84.4 %reduce-scatter.23.cloned.1.call-start = ((), (), s32[]{:S(2)}) async-start(), calls=%async_computation.16 | async-start | bytes 3932160 | tf_op jit(solution)/shard_map/reduce_scatter | solution.py:255
  546.4 74.3 %all-gather.14.cloned.1.call-start = ((), (), s32[]{:S(2)}) async-start(), calls=%async_computation.17 | async-start | bytes 3932160 | tf_op jit(solution)/shard_map/all_gather | solution.py:267
  592.0 278.3 %reduce-scatter.37.cloned.1.call-start = ((), (), s32[]{:S(2)}) async-start(), calls=%async_computation.24 | async-start | bytes 884736
  807.6 102.1 %reduce-scatter.25.cloned.1.call-start = ((), (), s32[]{:S(2)}) async-start(), calls=%async_computation.18 | async-start | bytes 3932160 | tf_op jit(solution)/shard_map/reduce_scatter | solution.py:299
  815.5 168.4 %reduce-scatter.29.cloned.1.call-start = ((), (), s32[]{:S(2)}) async-start(), calls=%async_computation.20 | async-start | bytes 2654208 | tf_op jit(solution)/shard_map/reduce_scatter | solution.py:348
  822.7 233.8 %reduce-scatter.27.cloned.1.call-start = ((), (), s32[]{:S(2)}) async-start(), calls=%async_computation.19 | async-start | bytes 2654208 | tf_op jit(solution)/shard_map/reduce_scatter | solution.py:347
  830.8 291.5 %reduce-scatter.31.cloned.1.call-start = ((), (), s32[]{:S(2)}) async-start(), calls=%async_computation.21 | async-start | bytes 884736
  836.8 350.9 %reduce-scatter.35.cloned.1.call-start = ((), (), s32[]{:S(2)}) async-start(), calls=%async_computation.23 | async-start | bytes 884736
  842.7 410.7 %reduce-scatter.33.cloned.1.call-start = ((), (), s32[]{:S(2)}) async-start(), calls=%async_computation.22 | async-start | bytes 884736
  849.0 63.5 %copy-start.34 = (f32[768]{0:T(1024)S(1)}, f32[768]{0:T(1024)}, u32[]{:S(2)}) copy-start(f32[768]{0:T(1024)} %get-tuple-element.409) | copy-start | bytes 9220
  849.0 63.5 %copy-start.35 = (f32[768]{0:T(1024)S(1)}, f32[768]{0:T(1024)}, u32[]{:S(2)}) copy-start(f32[768]{0:T(1024)} %get-tuple-element.413) | copy-start | bytes 9220
  849.0 63.5 %copy-start.36 = (f32[768]{0:T(1024)S(1)}, f32[768]{0:T(1024)}, u32[]{:S(2)}) copy-start(f32[768]{0:T(1024)} %get-tuple-element.407) | copy-start | bytes 9220
  849.0 63.5 %copy-start.37 = (f32[768]{0:T(1024)S(1)}, f32[768]{0:T(1024)}, u32[]{:S(2)}) copy-start(f32[768]{0:T(1024)} %get-tuple-element.411) | copy-start | bytes 9220
  849.1 63.5 %copy-start.38 = (f32[768]{0:T(1024)S(1)}, f32[768]{0:T(1024)}, u32[]{:S(2)}) copy-start(f32[768]{0:T(1024)} %get-tuple-element.412) | copy-start | bytes 9220
  849.1 110.4 %copy-start.2 = (f32[512,768]{1,0:T(8,128)S(1)}, f32[512,768]{1,0:T(8,128)}, u32[]{:S(2)}) copy-start(f32[512,768]{1,0:T(8,128)} %copy-done.1) | copy-start | bytes 4718596
  849.1 110.4 %copy-start.26 = (f32[512]{0:T(512)S(1)}, f32[512]{0:T(512)}, u32[]{:S(2)}) copy-start(f32[512]{0:T(512)} %copy-done.25) | copy-start | bytes 6148
  849.1 110.4 %copy-start.29 = (f32[768]{0:T(1024)S(1)}, f32[768]{0:T(1024)}, u32[]{:S(2)}) copy-start(f32[768]{0:T(1024)} %get-tuple-element.473) | copy-start | bytes 9220
  849.1 110.4 %copy-start.32 = (f32[512]{0:T(512)S(1)}, f32[512]{0:T(512)}, u32[]{:S(2)}) copy-start(f32[512]{0:T(512)} %copy-done.31) | copy-start | bytes 6148
  (54 other events, 308.3 us)
Sparse Core Ops, SparseCore 0:
  10.4 31.9 all-gather.5
  324.9 37.8 reduce-scatter.18
  457.6 36.4 reduce-scatter.20
  500.2 28.5 all-gather.11
  546.5 37.9 reduce-scatter.22
  592.1 28.5 all-gather.13
Sparse Core Ops, SparseCore 1:
  367.2 41.4 all-gather.7
  410.9 40.0 all-gather.9
  807.7 62.6 reduce-scatter.36
  872.8 36.8 reduce-scatter.24
  914.2 69.6 reduce-scatter.28
  988.3 68.1 reduce-scatter.26
  1060.6 61.6 reduce-scatter.30
  1126.1 61.6 reduce-scatter.34
  1191.8 61.5 reduce-scatter.32
